TPU v7x, 32 devices: a whole 2x2x4 slice. The times are simulated.
32 devices in a mesh: seq: 8 (over z, x), tp: 4 (over y, core).
Axes of the slice: x: 2, y: 2, z: 4, core: 2. Of those that a mesh axis runs over, the one named last changes fastest.
Arguments:
- tokens_in: bfloat16 [4, 16, 1024], replicated, may hold values from -6 to 6
- key_cache: bfloat16 [16, 2048, 1024], P(None, 'seq', 'tp'), may hold values from -6 to 6
- value_cache: bfloat16 [16, 2048, 1024], P(None, 'seq', 'tp'), may hold values from -6 to 6
- cache_len: int32 [16], replicated, may hold values from 1 to 2048, as said below
- bucket_table: int32 [2052], replicated, may hold values from 0 to 31, as said below
- rel_bias: float32 [32, 16], P(None, 'tp'), may hold values from -4 to 283
- attn_gain: float32 [1024], replicated, may hold values from 0.1 to 1.9
- moe_gain: float32 [1024], replicated, may hold values from 0.1 to 1.9
- w_qkv: bfloat16 [3, 1024, 1024], P(None, None, 'tp'), may hold values from -0.1875 to 0.1875
- w_out: bfloat16 [1024, 1024], P('tp'), may hold values from -0.1875 to 0.1875
- router: bfloat16 [1024, 16], replicated, may hold values from -0.1875 to 0.1875
- expert_choice: int32 [4, 16, 2], replicated, may hold values from 0 to 15, all different within a row
- w_gate_up: bfloat16 [2, 45056, 1024], P(None, ('seq', 'tp')), may hold values from -0.1875 to 0.1875
- w_down: bfloat16 [45056, 1024], P(('seq', 'tp')), may hold values from -0.109375 to 0.109375
Outputs:
- layer_out: bfloat16 [4, 16, 1024], replicated
Inputs may be any that keep to these rules, and one draw needn't show every extreme that they name: Request r's cache holds its positions 0 to cache_len[r] - 1; some request holds exactly 2048. `bucket_table`: non-decreasing in the distance, 0 at distance 0. `expert_choice`: the 2 experts of a token differ.
All inputs are finite; a program needn't handle non-finite values.
Results may differ from a plain program's by a relative error of at most 0.012.
Values sent between devices are 32-bit elements; how exact they have to be, the bound alone decides.
No kernel may reach another device: no remote copies, remote signals or barrier semaphores. Data moves between devices by JAX's collectives and lax.ppermute only.
A program may use at most 64 MiB of HBM per device.

v0:
```python
import jax
import jax.numpy as jnp
from jax import lax
from jax.sharding import PartitionSpec as P

HEAD_DIM = 64
FF = 2816
NEG = -1e30
EPS = 1e-06


def rms_scale(values, gain_vec):
    return values * lax.rsqrt(jnp.mean(values * values, axis=-1, keepdims=True) + EPS) * gain_vec


def on_device(
    tokens_in,
    key_cache,
    value_cache,
    cache_len,
    bucket_table,
    rel_bias,
    attn_gain,
    moe_gain,
    w_qkv,
    w_out,
    router,
    expert_choice,
    w_gate_up,
    w_down,
):
    steps_all, requests, model_width = tokens_in.shape
    cache_rows = key_cache.shape[1]
    heads_local = key_cache.shape[2] // HEAD_DIM
    table_len = bucket_table.shape[0]
    num_buckets = rel_bias.shape[0]
    num_experts = router.shape[1]
    hidden_local = w_down.shape[0]
    bucket_ids = jnp.arange(num_buckets, dtype=jnp.int32)

    def bias_lookup(buckets, pattern):
        onehot = (buckets[..., None] == bucket_ids).astype(jnp.float32)
        return jnp.einsum(pattern, onehot, rel_bias, precision=lax.Precision.HIGHEST)

    normed = rms_scale(tokens_in.astype(jnp.float32), attn_gain).astype(jnp.bfloat16)
    projected = jnp.einsum(
        "srd,kdf->ksrf", normed, w_qkv, preferred_element_type=jnp.float32
    ).astype(jnp.bfloat16)
    head_shape = (steps_all, requests, heads_local, HEAD_DIM)
    queries = projected[0].reshape(head_shape)
    fresh_keys = projected[1].reshape(head_shape)
    fresh_values = projected[2].reshape(head_shape)
    keys_heads = key_cache.reshape(requests, cache_rows, heads_local, HEAD_DIM)
    values_heads = value_cache.reshape(requests, cache_rows, heads_local, HEAD_DIM)
    positions = lax.axis_index("seq") * cache_rows + jnp.arange(cache_rows, dtype=jnp.int32)
    live_rows = positions[None, :] < cache_len[:, None]

    def cache_part(query_blk, step_ids, keys_blk, vals_blk, lens_blk, live_blk):
        scores = jnp.einsum(
            "srhd,rchd->srhc", query_blk, keys_blk, preferred_element_type=jnp.float32
        )
        distance = lens_blk[None, :, None] + step_ids[:, None, None] - positions[None, None, :]
        buckets = jnp.take(bucket_table, jnp.clip(distance, 0, table_len - 1))
        scores = scores + bias_lookup(buckets, "srcb,bh->srhc")
        usable = live_blk[None, :, None, :]
        scores = jnp.where(usable, scores, NEG)
        maxima = jnp.max(scores, axis=-1)
        weights = jnp.where(usable, jnp.exp(scores - maxima[..., None]), 0.0)
        summed = jnp.einsum(
            "srhc,rchd->srhd", weights, vals_blk, preferred_element_type=jnp.float32
        )
        return (maxima, jnp.sum(weights, axis=-1), summed)

    def attend_cache(query_blk, step_ids):
        return cache_part(query_blk, step_ids, keys_heads, values_heads, cache_len, live_rows)

    def merge_cache(maxima, totals, summed):
        overall = lax.pmax(maxima, "seq")
        factor = jnp.exp(maxima - overall)
        totals, summed = lax.psum((totals * factor, summed * factor[..., None]), "seq")
        return (overall, totals, summed)

    def attend_recent(query_blk, step_ids):
        scores = jnp.einsum(
            "srhd,jrhd->srhj", query_blk, fresh_keys, preferred_element_type=jnp.float32
        )
        distance = step_ids[:, None] - jnp.arange(steps_all, dtype=jnp.int32)[None, :]
        buckets = jnp.take(bucket_table, jnp.clip(distance, 0, table_len - 1))
        scores = scores + bias_lookup(buckets, "sjb,bh->shj")[:, None]
        usable = (distance >= 0)[:, None, None, :]
        scores = jnp.where(usable, scores, NEG)
        maxima = jnp.max(scores, axis=-1)
        weights = jnp.where(usable, jnp.exp(scores - maxima[..., None]), 0.0)
        summed = jnp.einsum(
            "srhj,jrhd->srhd", weights, fresh_values, preferred_element_type=jnp.float32
        )
        return (maxima, jnp.sum(weights, axis=-1), summed)

    first_col = (lax.axis_index("seq") * lax.axis_size("tp") + lax.axis_index("tp")) * hidden_local
    col_expert = (first_col + jnp.arange(hidden_local, dtype=jnp.int32)) // FF
    owner = (col_expert[None, :] == jnp.arange(num_experts, dtype=jnp.int32)[:, None]).astype(
        jnp.float32
    )

    def layer(start, step_count):
        step_ids = jnp.arange(start, start + step_count, dtype=jnp.int32)
        query_blk = queries[start : start + step_count]
        cache_max, cache_tot, cache_sum = merge_cache(*attend_cache(query_blk, step_ids))
        new_max, new_tot, new_sum = attend_recent(query_blk, step_ids)
        joint = jnp.maximum(cache_max, new_max)
        scale_cache = jnp.exp(cache_max - joint)
        scale_new = jnp.exp(new_max - joint)
        totals = cache_tot * scale_cache + new_tot * scale_new
        summed = cache_sum * scale_cache[..., None] + new_sum * scale_new[..., None]
        attended = (
            (summed / totals[..., None])
            .reshape(step_count, requests, heads_local * HEAD_DIM)
            .astype(jnp.bfloat16)
        )
        partial_value = jnp.einsum(
            "srf,fd->srd", attended, w_out, preferred_element_type=jnp.float32
        )
        mid = tokens_in[start : start + step_count].astype(jnp.float32) + lax.psum(
            partial_value, "tp"
        )
        moe_in = rms_scale(mid, moe_gain).astype(jnp.bfloat16)
        logits = jnp.einsum("srd,de->sre", moe_in, router, preferred_element_type=jnp.float32)
        picked = expert_choice[start : start + step_count][..., None] == jnp.arange(
            num_experts, dtype=jnp.int32
        )
        chosen = jnp.sum(jnp.where(picked, logits[:, :, None, :], 0.0), axis=-1)
        leading = jax.nn.sigmoid(chosen[..., 0] - chosen[..., 1])
        gate_pair = jnp.stack([leading, 1.0 - leading], axis=-1)
        per_expert = jnp.sum(jnp.where(picked, gate_pair[..., None], 0.0), axis=2)
        coef = jnp.einsum("sre,ef->srf", per_expert, owner, precision=lax.Precision.HIGHEST)
        gate_up = jnp.einsum("srd,kfd->ksrf", moe_in, w_gate_up, preferred_element_type=jnp.float32)
        hidden = (jax.nn.gelu(gate_up[0], approximate=True) * gate_up[1] * coef).astype(
            jnp.bfloat16
        )
        expert_part = jnp.einsum("srf,fd->srd", hidden, w_down, preferred_element_type=jnp.float32)
        mixture = lax.psum(expert_part, ("seq", "tp"))
        return (mid + mixture).astype(jnp.bfloat16)

    return layer(0, steps_all)


def solution(mesh):
    return jax.shard_map(
        on_device,
        mesh=mesh,
        in_specs=(
            P(),
            P(None, "seq", "tp"),
            P(None, "seq", "tp"),
            P(),
            P(),
            P(None, "tp"),
            P(),
            P(),
            P(None, None, "tp"),
            P("tp", None),
            P(),
            P(),
            P(None, ("seq", "tp"), None),
            P(("seq", "tp"), None),
        ),
        out_specs=P(),
        check_vma=False,
    )
```

profile of v0, /device:TPU:0, one launch (start us, length us, event | category | flops | bytes accessed | tf_op | source)
XLA Modules:
  0.0 400.7 jit_solution(13281460656458387013)
XLA Ops:
  6.5 0.0 copy-start
  6.5 0.0 all-reduce.4.cloned.1.call-start
  6.5 0.8 iota_add_fusion.1
  7.4 0.8 broadcast_compare_fusion
  8.2 0.1 compare_select_fusion
  8.3 0.0 copy-done.1
  8.3 0.0 copy-start.2
  8.3 0.0 copy-start.10
  8.3 90.5 %gather_fusion = s32[16384]{0:T(1024)S(1)} fusion(s32[2052]{0:T(1024)S(1)} %copy-done.1, s32[16384]{0:T(1024)S(1)} %broadcast_clamp_fusion), kind=kCustom, calls=%fused_computation | custom fusion | bytes 196608 | tf_op jit(solution)/shard_map/jit(_take)/gather | solution.py:63
  98.9 0.1 fusion.59
  99.0 0.0 copy-done.2
  99.0 0.1 fusion.37
  99.2 1.8 fusion.23
  101.0 0.6 fusion.78
  101.6 0.1 reshape_squeeze.9
  101.7 0.0 copy-start.6
  101.7 0.0 copy-start.13
  101.7 4.0 copy.81
  105.7 0.7 fusion.8
  106.4 2.1 fusion.80
  108.6 38.8 %pmax.7 = f32[4,16,4]{0,2,1:T(4,128)S(1)} all-reduce(f32[4,16,4]{0,2,1:T(4,128)S(1)} %get-tuple-element.17), channel_id=1, replica_groups=mesh['seq'=8,'tp'=4] {'seq'}, use_global_device_ids=true, to_apply=%region_2.3 | all-reduce | flops 256 | bytes 2048 | tf_op jit(solution)/shard_map/pmax | solution.py:78
  147.4 0.3 fusion.40
  147.7 3.9 copy.84
  151.7 3.0 fusion.16
  154.6 0.0 all-reduce.4.cloned.1.call-update
  154.7 0.0 all-reduce.6.cloned.1.call-start
  154.7 33.7 %psum.29 = f32[4,16,4]{0,2,1:T(4,128)} all-reduce(f32[4,16,4]{0,2,1:T(4,128)S(1)} %bitcast.133), channel_id=1, replica_groups=mesh['seq'=8,'tp'=4] {'seq'}, use_global_device_ids=true, to_apply=%region_6.7 | all-reduce | flops 256 | bytes 2048 | tf_op jit(solution)/shard_map/psum | solution.py:80
  188.4 0.7 reshape_squeeze.10
  189.1 0.1 copy.85
  189.2 0.1 reshape.206
  189.3 0.7 gather_fusion.1
  190.0 0.1 reshape.205
  190.1 0.2 convolution_bitcast_fusion.4
  190.3 0.1 copy.88
  190.4 1.2 fusion.81
  191.6 0.6 copy-done.7
  192.3 0.1 fusion.51
  192.4 1.4 multiply_add_fusion
  193.9 1.5 reshape_squeeze.11
  195.3 26.5 %all-reduce.4.cloned.1.call-done = f32[4,16,4,64]{3,0,2,1:T(4,128)} async-done(((f32[4,16,4,64]{3,0,2,1:T(4,128)}), f32[4,16,4,64]{3,0,2,1:T(4,128)}) %all-reduce.4.cloned.1.call-update) | async-done | bytes 65552 | tf_op jit(solution)/shard_map/psum | solution.py:80
  221.9 1.4 fusion.22
  223.2 0.7 copy.91
  223.9 1.6 convert_element_type.36
  225.5 1.7 fusion.27
  227.1 0.0 all-reduce.6.cloned.1.call-update
  227.1 0.0 all-reduce.8.cloned.1.call-start
  227.2 31.3 %all-reduce.6.cloned.1.call-done = f32[4,16,1024]{2,1,0:T(8,128)} async-done(((f32[4,16,1024]{2,1,0:T(8,128)}), f32[4,16,1024]{2,1,0:T(8,128)}) %all-reduce.6.cloned.1.call-update) | async-done | bytes 262160 | tf_op jit(solution)/shard_map/psum | solution.py:123
  258.5 1.1 multiply_reduce_fusion
  259.6 0.0 copy-done.12
  259.6 1.1 multiply_convert_fusion
  260.7 0.0 copy-start.9
  260.7 0.0 copy-start.11
  260.7 4.5 %fusion.4 = f32[2,4,16,1408]{3,2,0,1:T(8,128)S(1)} fusion(bf16[2,1408,1024]{2,1,0:T(8,128)(2,1)} %param.26, bf16[4,16,1024]{2,1,0:T(8,128)(2,1)S(1)} %multiply_convert_fusion), kind=kOutput, calls=%fused_computation.6 | convolution fusion | flops 369098752 | bytes 6619136 | tf_op jit(solution)/shard_map/srd,kfd->ksrf/dot_general | solution.py:136
  265.2 0.0 copy-done.9
  265.2 0.2 fusion.66
  265.4 0.0 copy-done.11
  265.4 0.2 select_reduce_fusion.1
  265.6 0.1 select_reduce_fusion
  265.7 0.3 fusion.7
  266.1 1.3 fusion.2
  267.4 0.0 all-reduce.8.cloned.1.call-update
  267.5 125.1 %all-reduce.8.cloned.1.call-done = f32[4,16,1024]{2,1,0:T(8,128)} async-done(((f32[4,16,1024]{2,1,0:T(8,128)}), f32[4,16,1024]{2,1,0:T(8,128)}) %all-reduce.8.cloned.1.call-update) | async-done | bytes 262160 | tf_op jit(solution)/shard_map/psum | solution.py:141
  392.5 0.0 copy-done.3
  392.5 1.6 add_convert_fusion
  (30 shorter events, 0.2 us)
Async XLA Ops:
  6.5 259.5 %copy-start = (bf16[1408,1024]{1,0:T(8,128)(2,1)S(1)}, bf16[1408,1024]{1,0:T(8,128)(2,1)}, u32[]{:S(2)}) copy-start(bf16[1408,1024]{1,0:T(8,128)(2,1)} %param.27) | copy-start | bytes 8650756
  6.5 1.8 copy-start.1
  6.5 215.3 %all-reduce.4.cloned.1.call-start = ((), (), s32[]{:S(2)}) async-start(), calls=%async_computation | async-start | bytes 262144 | tf_op jit(solution)/shard_map/psum | solution.py:80
  8.3 90.7 %copy-start.2 = (bf16[4,16,1024]{2,1,0:T(8,128)(2,1)S(1)}, bf16[4,16,1024]{2,1,0:T(8,128)(2,1)}, u32[]{:S(2)}) copy-start(bf16[4,16,1024]{2,1,0:T(8,128)(2,1)} %param.14) | copy-start | bytes 393220
  8.3 90.8 %copy-start.10 = (f32[1024]{0:T(1024)S(1)}, f32[1024]{0:T(1024)}, u32[]{:S(2)}) copy-start(f32[1024]{0:T(1024)} %param.20) | copy-start | bytes 12292
  101.7 4.7 %copy-start.6 = (bf16[4,16,4,64]{3,2,1,0:T(4,128)(2,1)}, bf16[4,16,4,64]{3,2,1,0:T(4,128)(2,1)S(1)}, u32[]{:S(2)}) copy-start(bf16[4,16,4,64]{3,2,1,0:T(4,128)(2,1)S(1)} %reshape_squeeze.9) | copy-start | bytes 98308
  101.7 4.0 copy-start.13
  147.4 4.2 %copy-start.5 = (f32[4,16,4]{0,2,1:T(4,128)}, f32[4,16,4]{0,2,1:T(4,128)S(1)}, u32[]{:S(2)}) copy-start(f32[4,16,4]{0,2,1:T(4,128)S(1)} %pmax.7) | copy-start | bytes 3076
  154.7 103.9 %all-reduce.6.cloned.1.call-start = ((), (), s32[]{:S(2)}) async-start(), calls=%async_computation.1 | async-start | bytes 524288 | tf_op jit(solution)/shard_map/psum | solution.py:123
  190.4 35.0 %copy-start.4 = (bf16[256,1024]{1,0:T(8,128)(2,1)S(1)}, bf16[256,1024]{1,0:T(8,128)(2,1)}, u32[]{:S(2)}) copy-start(bf16[256,1024]{1,0:T(8,128)(2,1)} %param.23) | copy-start | bytes 1572868
  191.6 0.7 copy-start.7
  191.6 0.8 copy-start.8
  221.9 37.8 %copy-start.12 = (f32[1024]{0:T(1024)S(1)}, f32[1024]{0:T(1024)}, u32[]{:S(2)}) copy-start(f32[1024]{0:T(1024)} %param.21) | copy-start | bytes 12292
  227.1 165.4 %all-reduce.8.cloned.1.call-start = ((), (), s32[]{:S(2)}) async-start(), calls=%async_computation.2 | async-start | bytes 524288 | tf_op jit(solution)/shard_map/psum | solution.py:141
  260.7 4.5 %copy-start.9 = (bf16[1024,16]{0,1:T(8,128)(2,1)S(1)}, bf16[1024,16]{0,1:T(8,128)(2,1)}, u32[]{:S(2)}) copy-start(bf16[1024,16]{0,1:T(8,128)(2,1)} %param.24) | copy-start | bytes 98308
  260.7 4.7 %copy-start.11 = (s32[4,16,2]{1,2,0:T(2,128)S(1)}, s32[4,16,2]{1,2,0:T(2,128)}, u32[]{:S(2)}) copy-start(s32[4,16,2]{1,2,0:T(2,128)} %param.25) | copy-start | bytes 1540
  266.1 126.5 %copy-start.3 = (f32[4,16,1024]{2,1,0:T(8,128)S(1)}, f32[4,16,1024]{2,1,0:T(8,128)}, u32[]{:S(2)}) copy-start(f32[4,16,1024]{2,1,0:T(8,128)} %all-reduce.6.cloned.1.call-done) | copy-start | bytes 786436
Sparse Core Ops, SparseCore 0:
  154.8 67.0 all-reduce.3
  227.3 31.2 all-reduce.5
  267.6 124.9 all-reduce.7
where the time goes:
time: 402 us; the launch traced here: 401 us
  waiting for transfers between devices  183 us (46%)
  local copies, waits for them, and re-layouts  105 us (26%)
  blocking collectives  72.5 us (18%)
  matrix products  18.5 us (5%)
  between operations  13.4 us (3%)
  other arithmetic  7.9 us (2%)
    psum x1, waiting for transfers between devices, layer(): mixture = lax.psum(expert_part, ('seq', 'tp'))  125 us
    gather x2, local copies, waits for them, and re-layouts, cache_part(): buckets = jnp.take(bucket_table, jnp.clip(distance, 0, table_len - 1))  90.6 us
    pmax x1, blocking collectives, merge_cache(): overall = lax.pmax(maxima, 'seq')  38.8 us
    psum x1, blocking collectives, merge_cache(): lax.psum((totals * factor, summed * factor[..., None]), 'seq')  33.7 us
    psum x1, waiting for transfers between devices, layer(): lax.psum(partial_value, 'tp')  31.3 us
    psum x1, waiting for transfers between devices, merge_cache(): lax.psum((totals * factor, summed * factor[..., None]), 'seq')  26.5 us
    unnamed x31, local copies, waits for them, and re-layouts  8.62 us
  transfers between devices with their start and end apart: 3, of which 3 were waited for; matrix products, arithmetic and copies ran while one was open for 2% of the time, Pallas kernels for 0%

commit v1 on v0

--- a/solution.py
+++ b/solution.py
@@ -138,7 +138,8 @@
             jnp.bfloat16
         )
         expert_part = jnp.einsum("srf,fd->srd", hidden, w_down, preferred_element_type=jnp.float32)
-        mixture = lax.psum(expert_part, ("seq", "tp"))
+        parts = lax.all_gather(expert_part, ("seq", "tp"), axis=0, tiled=False)
+        mixture = parts.sum(axis=0)
         return (mid + mixture).astype(jnp.bfloat16)
 
     return layer(0, steps_all)

time: 402 us -> 359 us (0.89)
  waiting for transfers between devices: 183 us -> 136 us
    psum x1 -> x0, waiting for transfers between devices: 125 us -> none  [layer(): mixture = lax.psum(expert_part, ('seq', 'tp'))]
    all_gather x0 -> x1, waiting for transfers between devices: none -> 77.7 us  [layer(): parts = lax.all_gather(expert_part, ('seq', 'tp'), axis=0, tiled=False)]
    reduce_sum x0 -> x1, other arithmetic: none -> 4.02 us  [layer(): mixture = parts.sum(axis=0)]
    unnamed x31 -> x29, local copies, waits for them, and re-layouts: 8.62 us -> 8.61 us
where the time goes in v1:
time: 359 us; the launch traced here: 358 us
  waiting for transfers between devices  136 us (38%)
  local copies, waits for them, and re-layouts  105 us (29%)
  blocking collectives  72.4 us (20%)
  matrix products  19.2 us (5%)
  between operations  13.4 us (4%)
  other arithmetic  11.9 us (3%)
    gather x2, local copies, waits for them, and re-layouts, cache_part(): buckets = jnp.take(bucket_table, jnp.clip(distance, 0, table_len - 1))  90.6 us
    all_gather x1, waiting for transfers between devices, layer(): parts = lax.all_gather(expert_part, ('seq', 'tp'), axis=0, tiled=False)  77.7 us
    pmax x1, blocking collectives, merge_cache(): overall = lax.pmax(maxima, 'seq')  38.8 us
    psum x1, blocking collectives, merge_cache(): lax.psum((totals * factor, summed * factor[..., None]), 'seq')  33.6 us
    psum x1, waiting for transfers between devices, layer(): lax.psum(partial_value, 'tp')  31.3 us
    psum x1, waiting for transfers between devices, merge_cache(): lax.psum((totals * factor, summed * factor[..., None]), 'seq')  26.6 us
    unnamed x29, local copies, waits for them, and re-layouts  8.61 us
  transfers between devices with their start and end apart: 3, of which 3 were waited for; matrix products, arithmetic and copies ran while one was open for 2% of the time, Pallas kernels for 0%

profile of v1, /device:TPU:0, one launch (start us, length us, event | category | flops | bytes accessed | tf_op | source)
XLA Modules:
  0.0 358.0 jit_solution(595871910778865491)
XLA Ops:
  6.5 0.0 copy-start
  6.5 0.0 all-reduce.3.cloned.1.call-start
  6.5 0.8 iota_add_fusion.1
  7.4 1.1 fusion.37
  8.5 0.7 broadcast_compare_fusion
  9.2 0.1 compare_select_fusion
  9.3 0.0 copy-done.1
  9.4 0.0 copy-start.2
  9.4 0.0 copy-start.9
  9.4 90.5 %gather_fusion = s32[16384]{0:T(1024)S(1)} fusion(s32[2052]{0:T(1024)S(1)} %copy-done.1, s32[16384]{0:T(1024)S(1)} %broadcast_clamp_fusion), kind=kCustom, calls=%fused_computation | custom fusion | bytes 196608 | tf_op jit(solution)/shard_map/jit(_take)/gather | solution.py:63
  100.0 0.1 fusion.59
  100.1 1.8 fusion.23
  101.9 0.6 fusion.78
  102.5 0.1 reshape_squeeze.9
  102.6 0.0 copy-start.6
  102.6 0.0 copy-start.12
  102.7 4.0 %copy.81 = bf16[16,256,256]{1,2,0:T(8,128)(2,1)} copy(bf16[16,256,256]{2,1,0:T(8,128)(2,1)} %param.15) | data formatting | bytes 4194304 | tf_op args[1]
  106.6 0.7 fusion.8
  107.4 2.1 fusion.80
  109.5 38.8 %pmax.7 = f32[4,16,4]{0,2,1:T(4,128)S(1)} all-reduce(f32[4,16,4]{0,2,1:T(4,128)S(1)} %get-tuple-element.17), channel_id=1, replica_groups=mesh['seq'=8,'tp'=4] {'seq'}, use_global_device_ids=true, to_apply=%region_2.3 | all-reduce | flops 256 | bytes 2048 | tf_op jit(solution)/shard_map/pmax | solution.py:78
  148.3 0.3 fusion.40
  148.6 3.9 %copy.84 = bf16[16,256,256]{1,2,0:T(8,128)(2,1)} copy(bf16[16,256,256]{2,1,0:T(8,128)(2,1)} %param.16) | data formatting | bytes 4194304 | tf_op args[2]
  152.6 0.0 copy-done.5
  152.6 3.0 fusion.16
  155.5 0.0 all-reduce.3.cloned.1.call-update
  155.6 0.0 all-reduce.5.cloned.1.call-start
  155.6 0.1 copy.85
  155.7 0.1 reshape.206
  155.8 0.7 gather_fusion.1
  156.5 0.1 reshape.205
  156.6 0.2 convolution_bitcast_fusion.4
  156.8 0.1 copy.88
  156.9 0.7 reshape_squeeze.10
  157.6 33.6 %psum.22 = f32[4,16,4]{0,2,1:T(4,128)} all-reduce(f32[4,16,4]{0,2,1:T(4,128)S(1)} %bitcast.134), channel_id=1, replica_groups=mesh['seq'=8,'tp'=4] {'seq'}, use_global_device_ids=true, to_apply=%region_6.7 | all-reduce | flops 256 | bytes 2048 | tf_op jit(solution)/shard_map/psum | solution.py:80
  191.3 1.2 fusion.81
  192.4 0.0 copy-start.7
  192.5 0.0 copy-start.8
  192.5 0.6 copy-done.7
  193.1 0.1 fusion.51
  193.2 1.4 multiply_add_fusion
  194.7 1.5 reshape_squeeze.11
  196.2 26.6 %all-reduce.3.cloned.1.call-done = f32[4,16,4,64]{3,0,2,1:T(4,128)} async-done(((f32[4,16,4,64]{3,0,2,1:T(4,128)}), f32[4,16,4,64]{3,0,2,1:T(4,128)}) %all-reduce.3.cloned.1.call-update) | async-done | bytes 65552 | tf_op jit(solution)/shard_map/psum | solution.py:80
  222.7 1.4 fusion.22
  224.1 0.7 copy.91
  224.8 1.6 convert_element_type.36
  226.4 1.7 fusion.27
  228.0 0.0 all-reduce.5.cloned.1.call-update
  228.0 0.0 all-gather.3.cloned.1.call-start
  228.1 31.3 %all-reduce.5.cloned.1.call-done = f32[4,16,1024]{2,1,0:T(8,128)} async-done(((f32[4,16,1024]{2,1,0:T(8,128)}), f32[4,16,1024]{2,1,0:T(8,128)}) %all-reduce.5.cloned.1.call-update) | async-done | bytes 262160 | tf_op jit(solution)/shard_map/psum | solution.py:123
  259.4 1.1 multiply_reduce_fusion
  260.5 0.0 copy-done.11
  260.5 1.1 multiply_convert_fusion
  261.6 0.9 fusion.66
  262.5 0.0 copy-done.10
  262.5 0.2 select_reduce_fusion.1
  262.7 0.1 select_reduce_fusion
  262.8 4.5 %fusion.4 = f32[2,4,16,1408]{3,2,0,1:T(8,128)S(1)} fusion(bf16[2,1408,1024]{2,1,0:T(8,128)(2,1)} %param.26, bf16[4,16,1024]{2,1,0:T(8,128)(2,1)S(1)} %multiply_convert_fusion), kind=kOutput, calls=%fused_computation.6 | convolution fusion | flops 369098752 | bytes 6619136 | tf_op jit(solution)/shard_map/srd,kfd->ksrf/dot_general | solution.py:136
  267.3 0.3 fusion.7
  267.7 0.0 copy-done
  267.7 1.3 fusion.2
  269.0 0.0 all-gather.3.cloned.1.call-update
  269.1 77.7 %all-gather.3.cloned.1.call-done = f32[128,16,1024]{2,1,0:T(8,128)} async-done(((f32[4,16,1024]{2,1,0:T(8,128)}), f32[128,16,1024]{2,1,0:T(8,128)}) %all-gather.3.cloned.1.call-update) | async-done | bytes 8388624 | tf_op jit(solution)/shard_map/all_gather | solution.py:141
  346.8 4.0 %reduce_sum.69 = f32[4,16,1024]{2,1,0:T(8,128)S(1)} reduce(f32[32,4,16,1024]{3,2,1,0:T(8,128)} %bitcast.126, f32[]{:T(128)} %constant.26.clone.1), dimensions={0}, to_apply=%region_12.13 | reduce | flops 2031616 | bytes 8650756 | tf_op jit(solution)/shard_map/reduce_sum | solution.py:142
  350.8 0.7 add_convert_fusion
  (29 shorter events, 0.2 us)
Async XLA Ops:
  6.5 261.2 %copy-start = (bf16[1408,1024]{1,0:T(8,128)(2,1)S(1)}, bf16[1408,1024]{1,0:T(8,128)(2,1)}, u32[]{:S(2)}) copy-start(bf16[1408,1024]{1,0:T(8,128)(2,1)} %param.27) | copy-start | bytes 8650756
  6.5 2.8 copy-start.1
  6.5 216.2 %all-reduce.3.cloned.1.call-start = ((), (), s32[]{:S(2)}) async-start(), calls=%async_computation | async-start | bytes 262144 | tf_op jit(solution)/shard_map/psum | solution.py:80
  9.4 90.7 %copy-start.2 = (bf16[4,16,1024]{2,1,0:T(8,128)(2,1)S(1)}, bf16[4,16,1024]{2,1,0:T(8,128)(2,1)}, u32[]{:S(2)}) copy-start(bf16[4,16,1024]{2,1,0:T(8,128)(2,1)} %param.14) | copy-start | bytes 393220
  9.4 90.7 %copy-start.9 = (f32[1024]{0:T(1024)S(1)}, f32[1024]{0:T(1024)}, u32[]{:S(2)}) copy-start(f32[1024]{0:T(1024)} %param.20) | copy-start | bytes 12292
  102.6 4.7 %copy-start.6 = (bf16[4,16,4,64]{3,2,1,0:T(4,128)(2,1)}, bf16[4,16,4,64]{3,2,1,0:T(4,128)(2,1)S(1)}, u32[]{:S(2)}) copy-start(bf16[4,16,4,64]{3,2,1,0:T(4,128)(2,1)S(1)} %reshape_squeeze.9) | copy-start | bytes 98308
  102.6 4.0 %copy-start.12 = (f32[32,4]{0,1:T(4,128)S(1)}, f32[32,4]{0,1:T(4,128)}, u32[]{:S(2)}) copy-start(f32[32,4]{0,1:T(4,128)} %param.19) | copy-start | bytes 1540
  148.3 4.2 %copy-start.5 = (f32[4,16,4]{0,2,1:T(4,128)}, f32[4,16,4]{0,2,1:T(4,128)S(1)}, u32[]{:S(2)}) copy-start(f32[4,16,4]{0,2,1:T(4,128)S(1)} %pmax.7) | copy-start | bytes 3076
  155.6 103.9 %all-reduce.5.cloned.1.call-start = ((), (), s32[]{:S(2)}) async-start(), calls=%async_computation.1 | async-start | bytes 524288 | tf_op jit(solution)/shard_map/psum | solution.py:123
  191.3 35.1 %copy-start.4 = (bf16[256,1024]{1,0:T(8,128)(2,1)S(1)}, bf16[256,1024]{1,0:T(8,128)(2,1)}, u32[]{:S(2)}) copy-start(bf16[256,1024]{1,0:T(8,128)(2,1)} %param.23) | copy-start | bytes 1572868
  192.4 0.7 copy-start.7
  192.5 0.8 copy-start.8
  222.7 37.8 %copy-start.11 = (f32[1024]{0:T(1024)S(1)}, f32[1024]{0:T(1024)}, u32[]{:S(2)}) copy-start(f32[1024]{0:T(1024)} %param.21) | copy-start | bytes 12292
  222.7 39.8 %copy-start.10 = (s32[4,16,2]{1,2,0:T(2,128)S(1)}, s32[4,16,2]{1,2,0:T(2,128)}, u32[]{:S(2)}) copy-start(s32[4,16,2]{1,2,0:T(2,128)} %param.25) | copy-start | bytes 1540
  228.0 118.7 %all-gather.3.cloned.1.call-start = ((), (), s32[]{:S(2)}) async-start(), calls=%async_computation.2 | async-start | bytes 8650752 | tf_op jit(solution)/shard_map/all_gather | solution.py:141
  346.8 4.0 %copy-start.3 = (f32[4,16,1024]{2,1,0:T(8,128)S(1)}, f32[4,16,1024]{2,1,0:T(8,128)}, u32[]{:S(2)}) copy-start(f32[4,16,1024]{2,1,0:T(8,128)} %all-reduce.5.cloned.1.call-done) | copy-start | bytes 786436
Sparse Core Ops, SparseCore 0:
  155.7 67.0 all-reduce.2
  228.2 31.2 all-reduce.4
  269.2 77.5 all-gather.2
